TPU v7x, 256 devices: a whole 4x4x8 slice. The times are simulated.
256 devices in a mesh: ctx: 32 (over y, z), ret: 2 (over core), tp: 4 (over x).
Axes of the slice: x: 4, y: 4, z: 8, core: 2. Of those that a mesh axis runs over, the one named last changes fastest.
Arguments:
- queries: bfloat16 [32768, 2048], P('ctx', 'tp'), may hold values from -256 to 256
- d_attn: bfloat16 [32768, 2048], P('ctx', 'tp'), may hold values from -6 to 6
- pool: bfloat16 [2, 32768, 896], P('ret', 'ctx'), may hold values from -6 to 6
- w_key: bfloat16 [896, 2048], P(None, 'tp'), may hold values from -0.1875 to 0.1875
- w_value: bfloat16 [896, 2048], P(None, 'tp'), may hold values from -0.1875 to 0.1875
- owners: int32 [512, 2], replicated, may hold values from 0 to 31, as said below
- picks: int32 [512, 2], replicated, may hold values from 0 to 1023
- live_counts: int32 [2, 32], replicated, may hold values from 1 to 8
Outputs:
- attn_out: bfloat16 [32768, 2048], P('ctx', 'tp')
- d_queries: bfloat16 [32768, 2048], P('ctx', 'tp')
- d_w_key: bfloat16 [896, 2048], P(None, 'tp')
- d_w_value: bfloat16 [896, 2048], P(None, 'tp')
Inputs may be any that keep to these rules, and one draw needn't show every extreme that they name: `owners`: in each column, at most 1 of the 16 spans of one ctx slab name the same owner, and in every slab some owner is named exactly 1 times.
All inputs are finite; a program needn't handle non-finite values.
Results may differ from a plain program's by a relative error of at most 0.0095.
The roundings to bfloat16 on the way count: a program that leaves them out, or rounds other values in their place, can miss the bound.
Values may be sent and summed in bfloat16 or wider, within the bound.
No kernel may reach another device: no remote copies, remote signals or barrier semaphores. Data moves between devices by JAX's collectives and lax.ppermute only.
A program may use at most 128 MiB of HBM per device.

v0:
```python
import math
import jax
import jax.numpy as jnp
from jax import lax
from jax.sharding import PartitionSpec as P

HEAD_DIM = 128
SPAN = 64
NBR_LEN = 128
CH_DEV = 16


def combined_all(x, axis, combine):
    everything = jax.tree.map(lambda part: lax.all_gather(part, axis), x)
    leading = jax.tree.map(lambda part: part[0], everything)

    def hop(k, so_far):
        return combine(so_far, jax.tree.map(lambda part: part[k], everything))

    return lax.fori_loop(1, lax.axis_size(axis), hop, leading)


def combine_stats(earlier, later):
    first_max, first_total = earlier
    second_max, second_total = later
    joint_max = jnp.maximum(first_max, second_max)
    joint_total = first_total * jnp.exp(first_max - joint_max) + second_total * jnp.exp(
        second_max - joint_max
    )
    return (joint_max, joint_total)


def body(queries, d_attn, pool, w_key, w_value, owners, picks, live_counts):
    ctx_count = lax.axis_size("ctx")
    ctx_place = lax.axis_index("ctx")
    ret_place = lax.axis_index("ret")
    capacity = (CH_DEV + ctx_count - 1) // ctx_count
    head_cols = w_key.shape[1]
    local_heads = head_cols // HEAD_DIM
    blocks = pool.shape[1] // NBR_LEN
    enc_width = pool.shape[2]
    score_scale = 1.0 / math.sqrt(HEAD_DIM)
    owner_col = lax.dynamic_index_in_dim(owners, ret_place, 1, keepdims=False)
    pick_col = lax.dynamic_index_in_dim(picks, ret_place, 1, keepdims=False)
    count_row = lax.dynamic_index_in_dim(live_counts, ret_place, 0, keepdims=False)
    owner_ids = jnp.arange(ctx_count, dtype=jnp.int32)
    counts_of = jnp.sum(
        jnp.where(owner_col[:, None] == owner_ids[None, :], count_row[None, :], 0), axis=1
    )
    slot_col = pick_col % counts_of
    owner_grid = owner_col.reshape(ctx_count, CH_DEV)
    slot_grid = slot_col.reshape(ctx_count, CH_DEV)
    position = jnp.arange(CH_DEV, dtype=jnp.int32)
    earlier = position[None, :] < position[:, None]
    same_owner = owner_grid[:, :, None] == owner_grid[:, None, :]
    request_rank = jnp.sum(jnp.logical_and(same_owner, earlier[None]), axis=2)
    places = jnp.arange(capacity, dtype=jnp.int32)
    wanted = jnp.logical_and(
        (owner_grid == ctx_place)[:, None, :], request_rank[:, None, :] == places[None, :, None]
    )
    send_slot = jnp.sum(jnp.where(wanted, slot_grid[:, None, :], 0), axis=2).reshape(-1)
    send_live = jnp.any(wanted, axis=2).reshape(-1)
    my_owner = lax.dynamic_index_in_dim(owner_grid, ctx_place, 0, keepdims=False)
    my_rank = lax.dynamic_index_in_dim(request_rank, ctx_place, 0, keepdims=False)
    recv_index = my_owner * capacity + my_rank
    pool_blocks = pool[0].reshape(blocks, NBR_LEN, enc_width)
    flat_pool = pool[0]
    own_keys = jnp.dot(flat_pool, w_key, preferred_element_type=jnp.float32).astype(jnp.bfloat16)
    own_values = jnp.dot(flat_pool, w_value, preferred_element_type=jnp.float32).astype(
        jnp.bfloat16
    )
    own_pair = jnp.concatenate([own_keys, own_values], axis=1).reshape(
        blocks, NBR_LEN, 2 * head_cols
    )
    outgoing = jnp.take(own_pair, send_slot, axis=0)
    incoming = lax.all_to_all(outgoing, "ctx", split_axis=0, concat_axis=0, tiled=True)
    chosen = jnp.take(incoming, recv_index, axis=0)
    key_tiles = chosen[:, :, :head_cols]
    value_tiles = chosen[:, :, head_cols:]
    query_tiles = queries.reshape(CH_DEV, SPAN, local_heads, HEAD_DIM)
    grad_out = d_attn.reshape(CH_DEV, SPAN, local_heads, HEAD_DIM)
    key_four = key_tiles.reshape(CH_DEV, NBR_LEN, local_heads, HEAD_DIM)
    value_four = value_tiles.reshape(CH_DEV, NBR_LEN, local_heads, HEAD_DIM)
    scores = (
        jnp.einsum("cmhd,clhd->chml", query_tiles, key_four, preferred_element_type=jnp.float32)
        * score_scale
    )
    local_max = jnp.max(scores, axis=3)
    local_total = jnp.sum(jnp.exp(scores - local_max[..., None]), axis=3)
    row_max, row_total = combined_all((local_max, local_total), "ret", combine_stats)
    attn_prob = jnp.exp(scores - row_max[..., None]) / row_total[..., None]
    prob_bf = attn_prob.astype(jnp.bfloat16)
    partial_value = jnp.einsum(
        "chml,clhd->cmhd", prob_bf, value_four, preferred_element_type=jnp.float32
    )
    attn_full = lax.psum(partial_value.reshape(CH_DEV * SPAN, head_cols), "ret")
    attn_out = attn_full.astype(jnp.bfloat16)
    out_dot = jnp.sum(
        grad_out.astype(jnp.float32)
        * attn_out.reshape(CH_DEV, SPAN, local_heads, HEAD_DIM).astype(jnp.float32),
        axis=3,
    )
    out_dot = jnp.transpose(out_dot, (0, 2, 1))
    grad_prob = jnp.einsum(
        "cmhd,clhd->chml", grad_out, value_four, preferred_element_type=jnp.float32
    )
    dscore = (attn_prob * (grad_prob - out_dot[..., None]) * score_scale).astype(jnp.bfloat16)
    dq_part = jnp.einsum("chml,clhd->cmhd", dscore, key_four, preferred_element_type=jnp.float32)
    d_queries = lax.psum(dq_part.reshape(CH_DEV * SPAN, head_cols), "ret").astype(jnp.bfloat16)
    key_grad = jnp.einsum(
        "chml,cmhd->clhd", dscore, query_tiles, preferred_element_type=jnp.float32
    ).astype(jnp.bfloat16)
    value_grad = jnp.einsum(
        "chml,cmhd->clhd", prob_bf, grad_out, preferred_element_type=jnp.float32
    ).astype(jnp.bfloat16)
    grad_pair = jnp.concatenate(
        [
            key_grad.reshape(CH_DEV, NBR_LEN, head_cols),
            value_grad.reshape(CH_DEV, NBR_LEN, head_cols),
        ],
        axis=2,
    )
    mean_share = 1.0 / (CH_DEV * ctx_count)
    back_hit = recv_index[None, :] == jnp.arange(ctx_count * capacity, dtype=jnp.int32)[:, None]
    back_span = jnp.sum(jnp.where(back_hit, position[None, :], 0), axis=1)
    returning = jnp.take(grad_pair, back_span, axis=0)
    arrived = lax.all_to_all(returning, "ctx", split_axis=0, concat_axis=0, tiled=True)
    arrived = arrived * send_live[:, None, None].astype(jnp.bfloat16)
    source = jnp.take(pool_blocks, send_slot, axis=0).reshape(-1, enc_width)
    weight_part = (
        jnp.einsum(
            "re,rk->ek",
            source,
            arrived.reshape(-1, 2 * head_cols),
            preferred_element_type=jnp.float32,
        )
        * mean_share
    )
    weight_sum = lax.psum(weight_part, ("ctx", "ret"))
    d_w_key = weight_sum[:, :head_cols].astype(jnp.bfloat16)
    d_w_value = weight_sum[:, head_cols:].astype(jnp.bfloat16)
    return (attn_out, d_queries, d_w_key, d_w_value)


def solution(mesh):
    return jax.shard_map(
        body,
        mesh=mesh,
        in_specs=(
            P("ctx", "tp"),
            P("ctx", "tp"),
            P("ret", "ctx", None),
            P(None, "tp"),
            P(None, "tp"),
            P(),
            P(),
            P(),
        ),
        out_specs=(P("ctx", "tp"), P("ctx", "tp"), P(None, "tp"), P(None, "tp")),
        check_vma=False,
    )
```

profile of v0, /device:TPU:2, one launch (start us, length us, event | category | flops | bytes accessed | tf_op | source)
XLA Modules:
  0.0 822.3 jit_solution(8104515446239602236)
XLA Ops:
  5.5 2.5 fusion.20
  10.8 4.0 copy.102
  14.8 6.5 gather_fusion
  21.3 7.5 broadcast_select_fusion.1
  28.8 11.7 %all-to-all-start = ((bf16[32,128,1024]{2,1,0:T(8,128)(2,1)}), bf16[32,128,1024]{2,1,0:T(8,128)(2,1)}, u32[]{:S(2)}, u32[]{:S(2)}) async-start(bf16[32,128,1024]{2,1,0:T(8,128)(2,1)} %broadcast_select_fusion.1), calls=%async_computation | async-start | bytes 16777216 | tf_op jit(solution)/shard_map/all_to_all | solution.py:76
  43.0 184.8 %all-to-all-done = bf16[32,128,1024]{2,1,0:T(8,128)(2,1)} async-done(((bf16[32,128,1024]{2,1,0:T(8,128)(2,1)}), bf16[32,128,1024]{2,1,0:T(8,128)(2,1)}, u32[]{:S(2)}, u32[]{:S(2)}) %all-to-all-start) | async-done | bytes 8388640 | tf_op jit(solution)/shard_map/all_to_all | solution.py:76
  227.8 6.2 gather_fusion.1
  234.0 2.6 broadcast_select_fusion.2
  236.6 2.5 fusion.45
  239.2 4.0 copy.82
  243.1 3.9 copy.81
  247.1 2.4 bitcast_reduce_fusion
  254.9 3.1 convolution_convert_fusion
  258.0 3.9 copy.95
  261.9 3.0 convolution_bitcast_fusion.1
  267.8 9.9 %all-reduce.3 = bf16[1024,512]{1,0:T(8,128)(2,1)} all-reduce(f32[1024,512]{1,0:T(8,128)} %bitcast.94), channel_id=1, replica_groups=mesh['ctx'=32,'ret'=2,'tp'=4] {'ret'}, use_global_device_ids=true, to_apply=%region_5.6 | all-reduce | flops 524288 | bytes 3145728 | tf_op jit(solution)/shard_map/psum | solution.py:96
  277.7 2.7 reshape.295
  280.5 3.0 multiply_reduce_fusion
  283.7 4.0 fusion.11
  287.7 2.1 convolution_convert_fusion.1
  289.8 3.9 copy.94
  293.8 4.8 pad_maximum_fusion
  298.5 7.1 gather_fusion.3
  305.6 7.5 broadcast_select_fusion
  313.1 13.5 %all-to-all-start.1 = ((bf16[32,128,1024]{2,1,0:T(8,128)(2,1)}), bf16[32,128,1024]{2,1,0:T(8,128)(2,1)}, u32[]{:S(2)}, u32[]{:S(2)}) async-start(bf16[32,128,1024]{2,1,0:T(8,128)(2,1)} %broadcast_select_fusion), calls=%async_computation.1 | async-start | bytes 16777216 | tf_op jit(solution)/shard_map/all_to_all | solution.py:127
  326.6 4.4 gather_fusion.2
  330.9 3.1 convolution_bitcast_fusion
  337.0 9.9 %all-reduce.4 = bf16[1024,512]{1,0:T(8,128)(2,1)} all-reduce(f32[1024,512]{1,0:T(8,128)} %bitcast.97), channel_id=1, replica_groups=mesh['ctx'=32,'ret'=2,'tp'=4] {'ret'}, use_global_device_ids=true, to_apply=%region_7.8 | all-reduce | flops 524288 | bytes 3145728 | tf_op jit(solution)/shard_map/psum | solution.py:109
  346.9 169.6 %all-to-all-done.1 = bf16[32,128,1024]{2,1,0:T(8,128)(2,1)} async-done(((bf16[32,128,1024]{2,1,0:T(8,128)(2,1)}), bf16[32,128,1024]{2,1,0:T(8,128)(2,1)}, u32[]{:S(2)}, u32[]{:S(2)}) %all-to-all-start.1) | async-done | bytes 8388640 | tf_op jit(solution)/shard_map/all_to_all | solution.py:127
  516.5 13.8 %bitcast_multiply_fusion = f32[896,1024]{1,0:T(8,128)} fusion(bf16[32,128,1024]{2,1,0:T(8,128)(2,1)} %all-to-all-done.1, bf16[32]{0:T(256)(128)(2,1)S(1)} %convert_element_type.66, bf16[32,128,896]{2,1,0:T(8,128)(2,1)} %gather_fusion.2, pred[32]{0:T(512)(128)(4,1)S(1)} %get-tuple-element.35), kind=kOutput, calls=%fused_computation.13 | convolution fusion | flops 7524974592 | bytes 19398752 | tf_op jit(solution)/shard_map/re,rk->ek/dot_general | solution.py:131
  530.3 289.2 %all-reduce.5 = bf16[896,1024]{1,0:T(8,128)(2,1)} all-reduce(f32[896,1024]{1,0:T(8,128)} %bitcast_multiply_fusion), channel_id=1, replica_groups=mesh['ctx'=32,'ret'=2,'tp'=4] {'ctx','ret'}, use_global_device_ids=true, to_apply=%region_10.11 | all-reduce | flops 917504 | bytes 5505024 | tf_op jit(solution)/shard_map/psum | solution.py:139
  819.5 2.8 fusion.46
  (55 shorter events, 21.5 us)
Async XLA Ops:
  0.6 4.8 copy-start
  5.4 2.6 copy-start.6
  28.7 11.7 %copy-start.5 = (bf16[1024,512]{1,0:T(8,128)(2,1)S(1)}, bf16[1024,512]{1,0:T(8,128)(2,1)}, u32[]{:S(2)}) copy-start(bf16[1024,512]{1,0:T(8,128)(2,1)} %param.9) | copy-start | bytes 3145732
  28.8 199.1 %all-to-all-start = ((bf16[32,128,1024]{2,1,0:T(8,128)(2,1)}), bf16[32,128,1024]{2,1,0:T(8,128)(2,1)}, u32[]{:S(2)}, u32[]{:S(2)}) async-start(bf16[32,128,1024]{2,1,0:T(8,128)(2,1)} %broadcast_select_fusion.1), calls=%async_computation | async-start | bytes 16777216 | tf_op jit(solution)/shard_map/all_to_all | solution.py:76
  249.4 8.5 %copy-start.1 = (f32[16,4,128,64]{2,3,1,0:T(8,128)}, f32[16,4,128,64]{2,3,1,0:T(8,128)S(1)}, u32[]{:S(2)}) copy-start(f32[16,4,128,64]{2,3,1,0:T(8,128)S(1)} %get-tuple-element.33) | copy-start | bytes 6291460
  249.5 5.4 copy-start.2
  287.7 2.1 copy-start.3
  313.1 203.5 %all-to-all-start.1 = ((bf16[32,128,1024]{2,1,0:T(8,128)(2,1)}), bf16[32,128,1024]{2,1,0:T(8,128)(2,1)}, u32[]{:S(2)}, u32[]{:S(2)}) async-start(bf16[32,128,1024]{2,1,0:T(8,128)(2,1)} %broadcast_select_fusion), calls=%async_computation.1 | async-start | bytes 16777216 | tf_op jit(solution)/shard_map/all_to_all | solution.py:127
  326.6 4.4 copy-start.4
where the time goes:
time: 823 us; the launch traced here: 822 us
  waiting for transfers between devices  354 us (43%)
  blocking collectives  313 us (38%)
  local copies, waits for them, and re-layouts  64.5 us (8%)
  matrix products  35.3 us (4%)
  other arithmetic  28.9 us (4%)
  starting transfers between devices  25.2 us (3%)
    psum x1, blocking collectives, body(): weight_sum = lax.psum(weight_part, ('ctx', 'ret'))  289 us
    all_to_all x1, waiting for transfers between devices, body(): lax.all_to_all(outgoing, 'ctx', split_axis=0, concat_axis=0, tiled=True)  185 us
    all_to_all x1, waiting for transfers between devices, body(): lax.all_to_all(returning, 'ctx', split_axis=0, concat_axis=0, tiled=True)  170 us
  transfers between devices with their start and end apart: 2, of which 2 were waited for; matrix products, arithmetic and copies ran while one was open for 2% of the time, Pallas kernels for 0%

commit v1 on v0

--- a/solution.py
+++ b/solution.py
@@ -136,7 +136,7 @@
         )
         * mean_share
     )
-    weight_sum = lax.psum(weight_part, ("ctx", "ret"))
+    weight_sum = lax.psum(lax.psum(weight_part, "ctx"), "ret")
     d_w_key = weight_sum[:, :head_cols].astype(jnp.bfloat16)
     d_w_value = weight_sum[:, head_cols:].astype(jnp.bfloat16)
     return (attn_out, d_queries, d_w_key, d_w_value)

time: 823 us -> 734 us (0.89)
  blocking collectives: 313 us -> 32.8 us
  waiting for transfers between devices: 354 us -> 529 us
  between operations: 0.92 us -> 14.3 us
    psum x1 -> x0, blocking collectives: 289 us -> none  [body(): weight_sum = lax.psum(weight_part, ('ctx', 'ret'))]
    psum x0 -> x1, waiting for transfers between devices: none -> 158 us  [body(): weight_sum = lax.psum(lax.psum(weight_part, 'ctx'), 'ret')]
    all_to_all x1, waiting for transfers between devices: 170 us -> 186 us  [body(): lax.all_to_all(returning, 'ctx', split_axis=0, concat_axis=0, tiled=True)]
    psum x1, blocking collectives: 9.89 us -> 18.9 us  [body(): lax.psum(dq_part.reshape(CH_DEV * SPAN, head_cols), 'ret')]
  transfers between devices with their start and end apart: 2 -> 3, of which waited for: 2 -> 3; matrix products, arithmetic and copies ran while one was open for 2% -> 2% of each run, Pallas kernels for 0% -> 0%
where the time goes in v1:
time: 734 us; the launch traced here: 731 us
  waiting for transfers between devices  529 us (72%)
  local copies, waits for them, and re-layouts  65.6 us (9%)
  matrix products  35.3 us (5%)
  blocking collectives  32.8 us (4%)
  other arithmetic  28.9 us (4%)
  starting transfers between devices  25.3 us (3%)
  between operations  14.3 us (2%)
    all_to_all x1, waiting for transfers between devices, body(): lax.all_to_all(returning, 'ctx', split_axis=0, concat_axis=0, tiled=True)  186 us
    all_to_all x1, waiting for transfers between devices, body(): lax.all_to_all(outgoing, 'ctx', split_axis=0, concat_axis=0, tiled=True)  185 us
    psum x1, waiting for transfers between devices, body(): weight_sum = lax.psum(lax.psum(weight_part, 'ctx'), 'ret')  158 us
    psum x1, blocking collectives, body(): lax.psum(dq_part.reshape(CH_DEV * SPAN, head_cols), 'ret')  18.9 us
  transfers between devices with their start and end apart: 3, of which 3 were waited for; matrix products, arithmetic and copies ran while one was open for 2% of the time, Pallas kernels for 0%

profile of v1, /device:TPU:2, one launch (start us, length us, event | category | flops | bytes accessed | tf_op | source)
XLA Modules:
  0.0 731.3 jit_solution(10146903338169970865)
XLA Ops:
  12.0 2.5 fusion.20
  17.3 4.0 copy.102
  21.3 6.5 gather_fusion
  27.8 7.5 %broadcast_select_fusion.1 = bf16[32,128,1024]{2,1,0:T(8,128)(2,1)} fusion(bf16[32,128,1024]{2,1,0:T(8,128)(2,1)} %gather_fusion, pred[32]{0:T(512)(128)(4,1)S(1)} %get-tuple-element.37), kind=kLoop, calls=%fused_computation.7 | loop fusion | flops 4194304 | bytes 16777248 | tf_op jit(solution)/shard_map/jit(_take)/select_n | solution.py:75
  35.3 11.7 %all-to-all-start = ((bf16[32,128,1024]{2,1,0:T(8,128)(2,1)}), bf16[32,128,1024]{2,1,0:T(8,128)(2,1)}, u32[]{:S(2)}, u32[]{:S(2)}) async-start(bf16[32,128,1024]{2,1,0:T(8,128)(2,1)} %broadcast_select_fusion.1), calls=%async_computation | async-start | bytes 16777216 | tf_op jit(solution)/shard_map/all_to_all | solution.py:76
  49.5 184.8 %all-to-all-done = bf16[32,128,1024]{2,1,0:T(8,128)(2,1)} async-done(((bf16[32,128,1024]{2,1,0:T(8,128)(2,1)}), bf16[32,128,1024]{2,1,0:T(8,128)(2,1)}, u32[]{:S(2)}, u32[]{:S(2)}) %all-to-all-start) | async-done | bytes 8388640 | tf_op jit(solution)/shard_map/all_to_all | solution.py:76
  234.4 6.2 gather_fusion.1
  240.5 2.6 broadcast_select_fusion.2
  243.2 2.5 fusion.45
  245.7 4.0 copy.82
  249.7 3.9 copy.81
  253.6 2.4 bitcast_reduce_fusion
  261.4 3.1 convolution_convert_fusion
  264.5 3.9 copy.95
  268.4 3.0 convolution_bitcast_fusion.1
  274.4 9.9 %all-reduce.6 = bf16[1024,512]{1,0:T(8,128)(2,1)} all-reduce(f32[1024,512]{1,0:T(8,128)} %bitcast.94), channel_id=1, replica_groups=mesh['ctx'=32,'ret'=2,'tp'=4] {'ret'}, use_global_device_ids=true, to_apply=%region_5.6 | all-reduce | flops 524288 | bytes 3145728 | tf_op jit(solution)/shard_map/psum | solution.py:96
  284.3 2.7 reshape.295
  287.0 3.0 multiply_reduce_fusion
  290.2 4.0 fusion.11
  294.2 2.1 convolution_convert_fusion.1
  296.4 3.9 copy.94
  300.3 4.8 pad_maximum_fusion
  305.0 7.1 gather_fusion.3
  312.1 7.5 %broadcast_select_fusion = bf16[32,128,1024]{2,1,0:T(8,128)(2,1)} fusion(bf16[32,128,1024]{2,1,0:T(8,128)(2,1)} %gather_fusion.3, pred[32]{0:T(512)(128)(4,1)S(1)} %get-tuple-element.36), kind=kLoop, calls=%fused_computation.6 | loop fusion | flops 4194304 | bytes 16777248 | tf_op jit(solution)/shard_map/jit(_take)/select_n | solution.py:126
  319.6 13.3 %all-to-all-start.1 = ((bf16[32,128,1024]{2,1,0:T(8,128)(2,1)}), bf16[32,128,1024]{2,1,0:T(8,128)(2,1)}, u32[]{:S(2)}, u32[]{:S(2)}) async-start(bf16[32,128,1024]{2,1,0:T(8,128)(2,1)} %broadcast_select_fusion), calls=%async_computation.1 | async-start | bytes 16777216 | tf_op jit(solution)/shard_map/all_to_all | solution.py:127
  333.2 4.4 gather_fusion.2
  337.5 186.2 %all-to-all-done.1 = bf16[32,128,1024]{2,1,0:T(8,128)(2,1)} async-done(((bf16[32,128,1024]{2,1,0:T(8,128)(2,1)}), bf16[32,128,1024]{2,1,0:T(8,128)(2,1)}, u32[]{:S(2)}, u32[]{:S(2)}) %all-to-all-start.1) | async-done | bytes 8388640 | tf_op jit(solution)/shard_map/all_to_all | solution.py:127
  523.7 13.8 %bitcast_multiply_fusion = f32[896,1024]{1,0:T(8,128)} fusion(bf16[32,128,1024]{2,1,0:T(8,128)(2,1)} %all-to-all-done.1, bf16[32]{0:T(256)(128)(2,1)S(1)} %convert_element_type.66, bf16[32,128,896]{2,1,0:T(8,128)(2,1)} %gather_fusion.2, pred[32]{0:T(512)(128)(4,1)S(1)} %get-tuple-element.37), kind=kOutput, calls=%fused_computation.13 | convolution fusion | flops 7524974592 | bytes 19398752 | tf_op jit(solution)/shard_map/re,rk->ek/dot_general | solution.py:131
  538.7 3.1 convolution_bitcast_fusion
  544.7 158.1 %all-reduce.5.cloned.1.call-done = f32[896,1024]{1,0:T(8,128)} async-done(((f32[896,1024]{1,0:T(8,128)}), f32[896,1024]{1,0:T(8,128)}) %all-reduce.5.cloned.1.call-update) | async-done | bytes 3670032 | tf_op jit(solution)/shard_map/psum | solution.py:139
  702.8 18.9 %all-reduce.7 = (bf16[1024,512]{1,0:T(8,128)(2,1)}, bf16[896,1024]{1,0:T(8,128)(2,1)}) all-reduce(f32[1024,512]{1,0:T(8,128)} %bitcast.97, f32[896,1024]{1,0:T(8,128)} %all-reduce.5.cloned.1.call-done), channel_id=1, replica_groups=mesh['ctx'=32,'ret'=2,'tp'=4] {'ret'}, use_global_device_ids=true, to_apply=%region_7.8 | all-reduce | flops 1441792 | bytes 8650752 | tf_op jit(solution)/shard_map/psum | solution.py:109
  721.6 2.8 fusion.46
  (57 shorter events, 22.9 us)
Async XLA Ops:
  7.2 4.8 copy-start
  12.0 2.6 copy-start.6
  35.3 11.7 %copy-start.5 = (bf16[1024,512]{1,0:T(8,128)(2,1)S(1)}, bf16[1024,512]{1,0:T(8,128)(2,1)}, u32[]{:S(2)}) copy-start(bf16[1024,512]{1,0:T(8,128)(2,1)} %param.9) | copy-start | bytes 3145732
  35.3 199.1 %all-to-all-start = ((bf16[32,128,1024]{2,1,0:T(8,128)(2,1)}), bf16[32,128,1024]{2,1,0:T(8,128)(2,1)}, u32[]{:S(2)}, u32[]{:S(2)}) async-start(bf16[32,128,1024]{2,1,0:T(8,128)(2,1)} %broadcast_select_fusion.1), calls=%async_computation | async-start | bytes 16777216 | tf_op jit(solution)/shard_map/all_to_all | solution.py:76
  256.0 8.5 %copy-start.1 = (f32[16,4,128,64]{2,3,1,0:T(8,128)}, f32[16,4,128,64]{2,3,1,0:T(8,128)S(1)}, u32[]{:S(2)}) copy-start(f32[16,4,128,64]{2,3,1,0:T(8,128)S(1)} %get-tuple-element.35) | copy-start | bytes 6291460
  256.0 5.4 copy-start.2
  294.2 2.1 copy-start.3
  319.6 204.1 %all-to-all-start.1 = ((bf16[32,128,1024]{2,1,0:T(8,128)(2,1)}), bf16[32,128,1024]{2,1,0:T(8,128)(2,1)}, u32[]{:S(2)}, u32[]{:S(2)}) async-start(bf16[32,128,1024]{2,1,0:T(8,128)(2,1)} %broadcast_select_fusion), calls=%async_computation.1 | async-start | bytes 16777216 | tf_op jit(solution)/shard_map/all_to_all | solution.py:127
  332.9 369.9 %all-reduce.5.cloned.1.call-start = ((), (), s32[]{:S(2)}) async-start(), calls=%async_computation.2 | async-start | bytes 7340032 | tf_op jit(solution)/shard_map/psum | solution.py:139
  537.4 1.2 copy-start.4
Sparse Core Ops, SparseCore 0:
  537.6 165.1 all-reduce.4
